TPU v7x, 32 devices: a whole 2x2x4 slice. The times are simulated.
32 devices in a mesh: group: 8 (over z, core), dev: 4 (over y, x).
Axes of the slice: x: 2, y: 2, z: 4, core: 2. Of those that a mesh axis runs over, the one named last changes fastest.
Arguments:
- tiles: bfloat16 [2304, 5, 128, 128], P(('group', 'dev')), may hold values from 0.00029945374 to 0.029907227
- tile_col: int32 [2304, 5], P(('group', 'dev')), may hold values from 0 to 15
- strip_group: int32 [2304], P(('group', 'dev')), may hold values from 0 to 7, as said below
- strip_slot: int32 [2304], P(('group', 'dev')), may hold values from 0 to 15
- live_count: int32 [32], P(('group', 'dev')), may hold values from 36 to 72, as said below
- omega: bfloat16 [16384, 128], P(('group', 'dev')), may hold values from -40 to 40
- idf: float32 [65536], P(('group', 'dev')), may hold values from 0.4 to 20
Outputs:
- q_basis: float32 [65536, 128], P(('group', 'dev'))
- doc_factor: bfloat16 [128, 16384], P(None, ('group', 'dev'))
Inputs may be any that keep to these rules, and one draw needn't show every extreme that they name: `strip_group`: among the 72 strips of one device at most 12 name one group; in every draw one group is named by exactly 12 strips of every device. `live_count`: some device has all 72 strips live.
All inputs are finite; a program needn't handle non-finite values.
Results may differ from a plain program's by a relative error of at most 0.0034.
Values may be sent and summed in bfloat16 or wider, within the bound.
No kernel may reach another device: no remote copies, remote signals or barrier semaphores. Data moves between devices by JAX's collectives and lax.ppermute only.
A program may use at most 128 MiB of HBM per device.

v0:
```python
import jax
import jax.numpy as jnp
from jax import lax
from jax.sharding import PartitionSpec as P


def on_device(tiles, tile_col, strip_group, strip_slot, live_count, omega, idf):
    n_group = lax.axis_size("group")
    n_dev = lax.axis_size("dev")
    strips = tiles.shape[0]
    tile_edge = tiles.shape[2]
    sketch_cols = omega.shape[1]
    owned_blocks = idf.shape[0] // tile_edge
    capacity = max(2, (4 * strips + 3 * n_group - 1) // (3 * n_group))
    alive_mask = (jnp.arange(strips) < live_count[0]).astype(jnp.float32)
    group_omega = lax.all_gather(omega, "dev", axis=0, tiled=True)
    omega_blocks = group_omega.reshape(-1, tile_edge, sketch_cols)
    picked = omega_blocks[tile_col]
    partial_value = jnp.einsum("stij,stjk->sik", tiles, picked, preferred_element_type=jnp.float32)
    partial_value = partial_value * alive_mask[:, None, None]
    member = (strip_group[:, None] == jnp.arange(n_group)[None, :]).astype(jnp.int32)
    rank_in = jnp.sum((jnp.cumsum(member, axis=0) - member) * member, axis=1)
    position = strip_group * capacity + rank_in
    labels = jnp.where(alive_mask > 0, strip_slot, -1).astype(jnp.float32)
    outgoing = (
        jnp.zeros((n_group * capacity, tile_edge, sketch_cols), jnp.float32)
        .at[position]
        .set(partial_value)
    )
    out_labels = jnp.full((n_group * capacity,), -1.0, jnp.float32).at[position].set(labels)
    arrived, arrived_labels = (
        lax.all_to_all(
            outgoing.reshape(n_group, capacity, tile_edge, sketch_cols),
            "group",
            split_axis=0,
            concat_axis=0,
            tiled=True,
        ),
        lax.all_to_all(
            out_labels.reshape(n_group, capacity), "group", split_axis=0, concat_axis=0, tiled=True
        ),
    )
    slot_ids = arrived_labels.reshape(-1).astype(jnp.int32)
    chooser = (jnp.arange(owned_blocks)[:, None] == slot_ids[None, :]).astype(jnp.float32)
    owned_rows = jnp.einsum(
        "rs,sik->rik",
        chooser,
        arrived.reshape(-1, tile_edge, sketch_cols),
        precision=lax.Precision.HIGHEST,
        preferred_element_type=jnp.float32,
    )
    sketch = owned_rows.reshape(-1, sketch_cols) * idf[:, None]
    total_terms = idf.shape[0] * n_group * n_dev
    local_gram = lax.dot_general(
        sketch,
        sketch,
        (((0,), (0,)), ((), ())),
        precision=lax.Precision.HIGHEST,
        preferred_element_type=jnp.float32,
    )
    gram_matrix = lax.psum(local_gram, ("group", "dev")) / total_terms
    lower_factor = jnp.linalg.cholesky(gram_matrix)
    q_basis = jax.scipy.linalg.solve_triangular(lower_factor, sketch.T, lower=True).T
    weighted = (
        (idf[:, None] * q_basis).astype(jnp.bfloat16).reshape(owned_blocks, tile_edge, sketch_cols)
    )
    band_rows = lax.all_gather(weighted, "group", axis=0, tiled=True)
    strip_q = band_rows[strip_group * owned_blocks + strip_slot]
    strip_q = strip_q * alive_mask.astype(jnp.bfloat16)[:, None, None]
    contrib = jnp.einsum("sik,stij->stkj", strip_q, tiles, preferred_element_type=jnp.float32)
    col_blocks = n_dev * (omega.shape[0] // tile_edge)
    doc_part = jax.ops.segment_sum(
        contrib.reshape(-1, sketch_cols, tile_edge), tile_col.reshape(-1), num_segments=col_blocks
    )
    my_docs = lax.psum_scatter(doc_part, "dev", scatter_dimension=0, tiled=True)
    doc_factor = jnp.transpose(my_docs, (1, 0, 2)).reshape(sketch_cols, -1).astype(jnp.bfloat16)
    return (q_basis, doc_factor)


def solution(mesh):
    placed = (
        P(("group", "dev"), None, None, None),
        P(("group", "dev"), None),
        P(("group", "dev")),
        P(("group", "dev")),
        P(("group", "dev")),
        P(("group", "dev"), None),
        P(("group", "dev")),
    )
    return jax.shard_map(
        on_device,
        mesh=mesh,
        in_specs=placed,
        out_specs=(P(("group", "dev"), None), P(None, ("group", "dev"))),
        check_vma=False,
    )
```

profile of v0, /device:TPU:0, one launch (start us, length us, event | category | flops | bytes accessed | tf_op | source)
XLA Modules:
  0.0 527.5 jit_solution(2830530185264732526)
XLA Ops:
  11.7 6.4 %all-to-all-start = ((f32[8,1,12]{2,1,0:T(1,128)}), f32[8,1,12]{2,1,0:T(1,128)S(1)}, u32[]{:S(2)}, u32[]{:S(2)}) async-start(f32[8,1,12]{2,1,0:T(1,128)} %bitcast.1), calls=%async_computation | async-start | bytes 8192 | tf_op jit(solution)/shard_map/all_to_all | solution.py:39
  18.0 11.5 %all_gather.6 = bf16[2048,128]{1,0:T(8,128)(2,1)S(1)} all-gather(bf16[512,128]{1,0:T(8,128)(2,1)} %param.12), channel_id=1, replica_groups=mesh['group'=8,'dev'=4] {'dev'}, dimensions={0}, use_global_device_ids=true | all-gather | bytes 655360 | tf_op jit(solution)/shard_map/all_gather | solution.py:16
  30.5 11.1 %gather_fusion = bf16[360,128,128]{2,1,0:T(8,128)(2,1)} fusion(bf16[16,128,128]{2,1,0:T(8,128)(2,1)S(1)} %bitcast.53, s32[1024]{0:T(1024)S(1)} %pad_clamp_fusion.1), kind=kCustom, calls=%fused_computation | custom fusion | bytes 23594400 | tf_op jit(solution)/shard_map/gather | solution.py:18
  41.6 11.8 %fusion.2 = f32[72,128,128]{1,2,0:T(8,128)} fusion(f32[72]{0:T(128)S(1)} %compare_convert_fusion, bf16[72,5,128,128]{3,2,1,0:T(8,128)(2,1)} %bitcast.55, bf16[72,5,128,128]{3,2,1,0:T(8,128)(2,1)} %param.7), kind=kOutput, calls=%fused_computation.8 | convolution fusion | flops 1511129088 | bytes 28311840 | tf_op jit(solution)/shard_map/stij,stjk->sik/dot_general | solution.py:19
  53.3 6.1 %copy.43 = f32[72,128,128]{2,1,0:T(8,128)} copy(f32[72,128,128]{1,2,0:T(8,128)} %fusion.2) | data formatting | bytes 9437184 | tf_op jit(solution)/shard_map/mul | solution.py:20
  59.4 3.4 broadcast_in_dim.36
  62.9 14.4 %scatter_fusion = f32[96,128,128]{2,1,0:T(8,128)} fusion(f32[96,128,128]{2,1,0:T(8,128)} %broadcast_in_dim.36, s32[72]{0:T(128)S(1)} %get-tuple-element.7, f32[72,128,128]{2,1,0:T(8,128)} %copy.43), kind=kCustom, calls=%fused_computation.3 | custom fusion | bytes 14156064 | tf_op jit(solution)/shard_map/scatter | solution.py:28
  77.3 4.9 all-to-all-start.1
  82.6 138.5 %all-to-all-done.1 = f32[8,12,128,128]{3,2,1,0:T(8,128)} async-done(((f32[8,12,128,128]{3,2,1,0:T(8,128)}), f32[8,12,128,128]{3,2,1,0:T(8,128)}, u32[]{:S(2)}, u32[]{:S(2)}) %all-to-all-start.1) | async-done | bytes 6291488 | tf_op jit(solution)/shard_map/all_to_all | solution.py:32
  221.1 8.3 %fusion.6 = f32[16,128,128]{2,0,1:T(8,128)S(1)} fusion(f32[96,128,128]{2,1,0:T(8,128)} %bitcast.9, f32[16,128]{0,1:T(8,128)S(1)} %copy.45, s32[96]{0:T(128)S(1)} %convert_element_type.50), kind=kOutput, calls=%fused_computation.12 | convolution fusion | flops 302253568 | bytes 7348608 | tf_op jit(solution)/shard_map/rs,sik->rik/dot_general | solution.py:45
  229.4 2.4 convolution_bitcast_fusion
  232.5 116.9 %all-reduce.2.cloned.1.call-done = f32[128,128]{0,1:T(8,128)} async-done(((f32[128,128]{0,1:T(8,128)}), f32[128,128]{0,1:T(8,128)}) %all-reduce.2.cloned.1.call-update) | async-done | bytes 65552 | tf_op jit(solution)/shard_map/psum | solution.py:61
  349.4 0.8 broadcast_multiply_fusion
  350.4 0.9 fusion.13
  351.2 11.7 %cholesky.16 = f32[128,128]{1,0:T(8,128)S(1)} custom-call(f32[128,128]{1,0:T(8,128)S(1)} %fusion.13), custom_call_target="Cholesky" | custom-call | tf_op jit(solution)/shard_map/jit(cholesky)/cholesky | solution.py:62
  364.3 9.8 %custom-call.7 = f32[1,128,128]{1,2,0:T(8,128)S(1)} custom-call(f32[1,128,128]{2,1,0:T(8,128)S(1)} %fusion.10), custom_call_target="InvertDiagBlocksLowerTriangular" | custom-call | tf_op jit(solution)/shard_map/jit(_solve_triangular)/triangular_solve | solution.py:63
  374.1 2.1 multiply_convert_fusion
  376.8 47.7 %all-gather.2.cloned.1.call-done = bf16[128,128,128]{2,1,0:T(8,128)(2,1)} async-done(((bf16[16,128,128]{2,1,0:T(8,128)(2,1)}), bf16[128,128,128]{2,1,0:T(8,128)(2,1)}) %all-gather.2.cloned.1.call-update) | async-done | bytes 4194320 | tf_op jit(solution)/shard_map/all_gather | solution.py:67
  424.5 3.2 gather_fusion.1
  427.7 15.5 %fusion.3 = f32[72,128,5,128]{3,1,2,0:T(8,128)} fusion(bf16[72,5,128,128]{3,2,1,0:T(8,128)(2,1)} %param.7, bf16[72,128,128]{2,1,0:T(8,128)(2,1)S(1)} %gather_fusion.1, bf16[72]{0:T(256)(128)(2,1)S(1)} %fusion.21), kind=kOutput, calls=%fused_computation.9 | convolution fusion | flops 1514668032 | bytes 37748880 | tf_op jit(solution)/shard_map/sik,stij->stkj/dot_general | solution.py:70
  443.3 47.9 %scatter_fusion.1 = f32[16,128,128]{2,1,0:T(8,128)S(1)} fusion(f32[16,128,128]{2,1,0:T(8,128)S(1)} %broadcast_in_dim.38, s32[360]{0:T(512)S(1)} %reshape.109, f32[360,128,128]{2,1,0:T(8,128)} %bitcast.54), kind=kCustom, calls=%fused_computation.4 | custom fusion | flops 5898240 | bytes 70780320 | tf_op jit(solution)/shard_map/scatter-add | solution.py:72
  491.2 1.0 copy-done
  492.2 26.9 %reduce-scatter.2.cloned.1.call-done = f32[4,128,128]{2,1,0:T(8,128)} async-done(((f32[16,128,128]{2,1,0:T(8,128)}), f32[4,128,128]{2,1,0:T(8,128)}) %reduce-scatter.2.cloned.1.call-update) | async-done | bytes 262160 | tf_op jit(solution)/shard_map/reduce_scatter | solution.py:75
  519.1 1.0 convert_bitcast_fusion
  (38 shorter events, 8.8 us)
Async XLA Ops:
  11.7 65.6 %all-to-all-start = ((f32[8,1,12]{2,1,0:T(1,128)}), f32[8,1,12]{2,1,0:T(1,128)S(1)}, u32[]{:S(2)}, u32[]{:S(2)}) async-start(f32[8,1,12]{2,1,0:T(1,128)} %bitcast.1), calls=%async_computation | async-start | bytes 8192 | tf_op jit(solution)/shard_map/all_to_all | solution.py:39
  77.3 5.1 copy-start.1
  77.3 143.8 %all-to-all-start.1 = ((f32[8,12,128,128]{3,2,1,0:T(8,128)}), f32[8,12,128,128]{3,2,1,0:T(8,128)}, u32[]{:S(2)}, u32[]{:S(2)}) async-start(f32[8,12,128,128]{3,2,1,0:T(8,128)} %bitcast.56), calls=%async_computation.1 | async-start | bytes 12582912 | tf_op jit(solution)/shard_map/all_to_all | solution.py:32
  82.2 267.2 %all-reduce.2.cloned.1.call-start = ((), (), s32[]{:S(2)}) async-start(), calls=%async_computation.3 | async-start | bytes 131072 | tf_op jit(solution)/shard_map/psum | solution.py:61
  221.1 155.4 %copy-start.2 = (s32[72,5]{0,1:T(8,128)S(1)}, s32[72,5]{0,1:T(8,128)}, u32[]{:S(2)}) copy-start(s32[72,5]{0,1:T(8,128)} %param.8) | copy-start | bytes 4324
  231.9 192.6 %all-gather.2.cloned.1.call-start = ((), (), s32[]{:S(2)}) async-start(), calls=%async_computation.4 | async-start | bytes 4718592 | tf_op jit(solution)/shard_map/all_gather | solution.py:67
  376.2 142.9 %reduce-scatter.2.cloned.1.call-start = ((), (), s32[]{:S(2)}) async-start(), calls=%async_computation.5 | async-start | bytes 1310720 | tf_op jit(solution)/shard_map/reduce_scatter | solution.py:75
  491.2 1.0 copy-start
Sparse Core Ops, SparseCore 0:
  232.0 117.3 all-reduce.1
  376.4 48.1 all-gather.1
  492.3 26.7 reduce-scatter.1
where the time goes:
time: 529 us; the launch traced here: 528 us
  waiting for transfers between devices  330 us (62%)
  other arithmetic  76.5 us (14%)
  local copies, waits for them, and re-layouts  42.8 us (8%)
  matrix products  40.1 us (8%)
  between operations  14.6 us (3%)
  starting transfers between devices  12 us (2%)
  blocking collectives  11.5 us (2%)
    all_to_all x1, waiting for transfers between devices, on_device(): lax.all_to_all(outgoing.reshape(n_group, capacity, tile_edge, sketch_cols...  138 us
    psum x1, waiting for transfers between devices, on_device(): gram_matrix = lax.psum(local_gram, ('group', 'dev')) / total_terms  117 us
    scatter-add x1, other arithmetic, on_device(): jax.ops.segment_sum(contrib.reshape(-1, sketch_cols, tile_edge), tile_col...  47.9 us
    all_gather x1, waiting for transfers between devices, on_device(): band_rows = lax.all_gather(weighted, 'group', axis=0, tiled=True)  47.7 us
    reduce_scatter x1, waiting for transfers between devices, on_device(): my_docs = lax.psum_scatter(doc_part, 'dev', scatter_dimension=0, tiled=True)  26.9 us
    dot_general x1, matrix products, on_device(): jnp.einsum('sik,stij->stkj', strip_q, tiles, preferred_element_type=jnp.f...  15.5 us
    scatter x1, local copies, waits for them, and re-layouts, on_device(): outgoing = jnp.zeros((n_group * capacity, tile_edge, sketch_cols), jnp.fl...  14.4 us
    another operation x3, other arithmetic, on_device(): lower_factor = jnp.linalg.cholesky(gram_matrix)  12.4 us
  transfers between devices with their start and end apart: 5, of which 4 were waited for; matrix products, arithmetic and copies ran while one was open for 9% of the time, Pallas kernels for 0%

commit v1 on v0

--- a/solution.py
+++ b/solution.py
@@ -58,7 +58,9 @@
         precision=lax.Precision.HIGHEST,
         preferred_element_type=jnp.float32,
     )
-    gram_matrix = lax.psum(local_gram, ("group", "dev")) / total_terms
+    gram_matrix = (
+        jax.lax.psum(jax.lax.psum(local_gram, axis_name="dev"), axis_name="group") / total_terms
+    )
     lower_factor = jnp.linalg.cholesky(gram_matrix)
     q_basis = jax.scipy.linalg.solve_triangular(lower_factor, sketch.T, lower=True).T
     weighted = (

time: 529 us -> 507 us (0.958)
  waiting for transfers between devices: 330 us -> 307 us
    psum x1 -> x2, waiting for transfers between devices: 117 us -> 96.3 us  [the longest x1 56.4 us: on_device(): jax.lax.psum(jax.lax.psum(local_gram, axis_name='dev'), axis_name='group')]
  transfers between devices with their start and end apart: 5 -> 6, of which waited for: 4 -> 5; matrix products, arithmetic and copies ran while one was open for 9% -> 10% of each run, Pallas kernels for 0% -> 0%
where the time goes in v1:
time: 507 us; the launch traced here: 505 us
  waiting for transfers between devices  307 us (61%)
  other arithmetic  76.5 us (15%)
  local copies, waits for them, and re-layouts  42.8 us (8%)
  matrix products  40.1 us (8%)
  between operations  14.6 us (3%)
  starting transfers between devices  12.1 us (2%)
  blocking collectives  11.5 us (2%)
    all_to_all x1, waiting for transfers between devices, on_device(): lax.all_to_all(outgoing.reshape(n_group, capacity, tile_edge, sketch_cols...  138 us
    psum x1, waiting for transfers between devices, on_device(): jax.lax.psum(jax.lax.psum(local_gram, axis_name='dev'), axis_name='group')  56.4 us
    scatter-add x1, other arithmetic, on_device(): jax.ops.segment_sum(contrib.reshape(-1, sketch_cols, tile_edge), tile_col...  47.9 us
    all_gather x1, waiting for transfers between devices, on_device(): band_rows = lax.all_gather(weighted, 'group', axis=0, tiled=True)  45.5 us
    psum x1, waiting for transfers between devices, on_device(): jax.lax.psum(local_gram, axis_name='dev')  39.9 us
    reduce_scatter x1, waiting for transfers between devices, on_device(): my_docs = lax.psum_scatter(doc_part, 'dev', scatter_dimension=0, tiled=True)  26.9 us
    dot_general x1, matrix products, on_device(): jnp.einsum('sik,stij->stkj', strip_q, tiles, preferred_element_type=jnp.f...  15.5 us
    scatter x1, local copies, waits for them, and re-layouts, on_device(): outgoing = jnp.zeros((n_group * capacity, tile_edge, sketch_cols), jnp.fl...  14.4 us
  transfers between devices with their start and end apart: 6, of which 5 were waited for; matrix products, arithmetic and copies ran while one was open for 10% of the time, Pallas kernels for 0%

profile of v1, /device:TPU:0, one launch (start us, length us, event | category | flops | bytes accessed | tf_op | source)
XLA Modules:
  0.0 504.8 jit_solution(2964049566211567149)
XLA Ops:
  11.7 6.4 %all-to-all-start = ((f32[8,1,12]{2,1,0:T(1,128)}), f32[8,1,12]{2,1,0:T(1,128)S(1)}, u32[]{:S(2)}, u32[]{:S(2)}) async-start(f32[8,1,12]{2,1,0:T(1,128)} %bitcast.1), calls=%async_computation | async-start | bytes 8192 | tf_op jit(solution)/shard_map/all_to_all | solution.py:39
  18.0 11.5 %all_gather.6 = bf16[2048,128]{1,0:T(8,128)(2,1)S(1)} all-gather(bf16[512,128]{1,0:T(8,128)(2,1)} %param.12), channel_id=1, replica_groups=mesh['group'=8,'dev'=4] {'dev'}, dimensions={0}, use_global_device_ids=true | all-gather | bytes 655360 | tf_op jit(solution)/shard_map/all_gather | solution.py:16
  30.5 11.1 %gather_fusion = bf16[360,128,128]{2,1,0:T(8,128)(2,1)} fusion(bf16[16,128,128]{2,1,0:T(8,128)(2,1)S(1)} %bitcast.53, s32[1024]{0:T(1024)S(1)} %pad_clamp_fusion.1), kind=kCustom, calls=%fused_computation | custom fusion | bytes 23594400 | tf_op jit(solution)/shard_map/gather | solution.py:18
  41.6 11.8 %fusion.2 = f32[72,128,128]{1,2,0:T(8,128)} fusion(f32[72]{0:T(128)S(1)} %compare_convert_fusion, bf16[72,5,128,128]{3,2,1,0:T(8,128)(2,1)} %bitcast.55, bf16[72,5,128,128]{3,2,1,0:T(8,128)(2,1)} %param.7), kind=kOutput, calls=%fused_computation.8 | convolution fusion | flops 1511129088 | bytes 28311840 | tf_op jit(solution)/shard_map/stij,stjk->sik/dot_general | solution.py:19
  53.3 6.1 %copy.43 = f32[72,128,128]{2,1,0:T(8,128)} copy(f32[72,128,128]{1,2,0:T(8,128)} %fusion.2) | data formatting | bytes 9437184 | tf_op jit(solution)/shard_map/mul | solution.py:20
  59.4 3.4 broadcast_in_dim.36
  62.9 14.4 %scatter_fusion = f32[96,128,128]{2,1,0:T(8,128)} fusion(f32[96,128,128]{2,1,0:T(8,128)} %broadcast_in_dim.36, s32[72]{0:T(128)S(1)} %get-tuple-element.7, f32[72,128,128]{2,1,0:T(8,128)} %copy.43), kind=kCustom, calls=%fused_computation.3 | custom fusion | bytes 14156064 | tf_op jit(solution)/shard_map/scatter | solution.py:28
  77.3 4.9 all-to-all-start.1
  82.6 138.5 %all-to-all-done.1 = f32[8,12,128,128]{3,2,1,0:T(8,128)} async-done(((f32[8,12,128,128]{3,2,1,0:T(8,128)}), f32[8,12,128,128]{3,2,1,0:T(8,128)}, u32[]{:S(2)}, u32[]{:S(2)}) %all-to-all-start.1) | async-done | bytes 6291488 | tf_op jit(solution)/shard_map/all_to_all | solution.py:32
  221.1 8.3 %fusion.6 = f32[16,128,128]{2,0,1:T(8,128)S(1)} fusion(f32[96,128,128]{2,1,0:T(8,128)} %bitcast.9, f32[16,128]{0,1:T(8,128)S(1)} %copy.45, s32[96]{0:T(128)S(1)} %convert_element_type.50), kind=kOutput, calls=%fused_computation.12 | convolution fusion | flops 302253568 | bytes 7348608 | tf_op jit(solution)/shard_map/rs,sik->rik/dot_general | solution.py:45
  229.4 2.4 convolution_bitcast_fusion
  232.0 39.9 %all-reduce.3.cloned.1.call-done = f32[128,128]{0,1:T(8,128)} async-done(((f32[128,128]{0,1:T(8,128)}), f32[128,128]{0,1:T(8,128)}) %all-reduce.3.cloned.1.call-update) | async-done | bytes 65552 | tf_op jit(solution)/shard_map/psum | solution.py:62
  272.5 56.4 %all-reduce.5.cloned.1.call-done = f32[128,128]{0,1:T(8,128)} async-done(((f32[128,128]{0,1:T(8,128)}), f32[128,128]{0,1:T(8,128)}) %all-reduce.5.cloned.1.call-update) | async-done | bytes 65552 | tf_op jit(solution)/shard_map/psum | solution.py:62
  329.9 0.9 fusion.13
  330.7 11.7 %cholesky.16 = f32[128,128]{1,0:T(8,128)S(1)} custom-call(f32[128,128]{1,0:T(8,128)S(1)} %fusion.13), custom_call_target="Cholesky" | custom-call | tf_op jit(solution)/shard_map/jit(cholesky)/cholesky | solution.py:64
  343.8 9.8 %custom-call.7 = f32[1,128,128]{1,2,0:T(8,128)S(1)} custom-call(f32[1,128,128]{2,1,0:T(8,128)S(1)} %fusion.10), custom_call_target="InvertDiagBlocksLowerTriangular" | custom-call | tf_op jit(solution)/shard_map/jit(_solve_triangular)/triangular_solve | solution.py:65
  353.6 2.1 multiply_convert_fusion
  356.3 45.5 %all-gather.2.cloned.1.call-done = bf16[128,128,128]{2,1,0:T(8,128)(2,1)} async-done(((bf16[16,128,128]{2,1,0:T(8,128)(2,1)}), bf16[128,128,128]{2,1,0:T(8,128)(2,1)}) %all-gather.2.cloned.1.call-update) | async-done | bytes 4194320 | tf_op jit(solution)/shard_map/all_gather | solution.py:69
  401.8 3.2 gather_fusion.1
  405.0 15.5 %fusion.3 = f32[72,128,5,128]{3,1,2,0:T(8,128)} fusion(bf16[72,5,128,128]{3,2,1,0:T(8,128)(2,1)} %param.7, bf16[72,128,128]{2,1,0:T(8,128)(2,1)S(1)} %gather_fusion.1, bf16[72]{0:T(256)(128)(2,1)S(1)} %fusion.21), kind=kOutput, calls=%fused_computation.9 | convolution fusion | flops 1514668032 | bytes 37748880 | tf_op jit(solution)/shard_map/sik,stij->stkj/dot_general | solution.py:72
  420.6 47.9 %scatter_fusion.1 = f32[16,128,128]{2,1,0:T(8,128)S(1)} fusion(f32[16,128,128]{2,1,0:T(8,128)S(1)} %broadcast_in_dim.38, s32[360]{0:T(512)S(1)} %reshape.109, f32[360,128,128]{2,1,0:T(8,128)} %bitcast.54), kind=kCustom, calls=%fused_computation.4 | custom fusion | flops 5898240 | bytes 70780320 | tf_op jit(solution)/shard_map/scatter-add | solution.py:74
  468.5 1.0 copy-done
  469.5 26.9 %reduce-scatter.2.cloned.1.call-done = f32[4,128,128]{2,1,0:T(8,128)} async-done(((f32[16,128,128]{2,1,0:T(8,128)}), f32[4,128,128]{2,1,0:T(8,128)}) %reduce-scatter.2.cloned.1.call-update) | async-done | bytes 262160 | tf_op jit(solution)/shard_map/reduce_scatter | solution.py:77
  496.4 1.0 convert_bitcast_fusion
  (41 shorter events, 9.7 us)
Async XLA Ops:
  11.7 65.6 %all-to-all-start = ((f32[8,1,12]{2,1,0:T(1,128)}), f32[8,1,12]{2,1,0:T(1,128)S(1)}, u32[]{:S(2)}, u32[]{:S(2)}) async-start(f32[8,1,12]{2,1,0:T(1,128)} %bitcast.1), calls=%async_computation | async-start | bytes 8192 | tf_op jit(solution)/shard_map/all_to_all | solution.py:39
  77.3 5.1 %copy-start.1 = (f32[2048]{0:T(1024)S(1)}, f32[2048]{0:T(1024)}, u32[]{:S(2)}) copy-start(f32[2048]{0:T(1024)} %param.13) | copy-start | bytes 24580
  77.3 143.8 %all-to-all-start.1 = ((f32[8,12,128,128]{3,2,1,0:T(8,128)}), f32[8,12,128,128]{3,2,1,0:T(8,128)}, u32[]{:S(2)}, u32[]{:S(2)}) async-start(f32[8,12,128,128]{3,2,1,0:T(8,128)} %bitcast.56), calls=%async_computation.1 | async-start | bytes 12582912 | tf_op jit(solution)/shard_map/all_to_all | solution.py:32
  82.2 189.7 %all-reduce.3.cloned.1.call-start = ((), (), s32[]{:S(2)}) async-start(), calls=%async_computation.3 | async-start | bytes 131072 | tf_op jit(solution)/shard_map/psum | solution.py:62
  221.1 134.9 %copy-start.2 = (s32[72,5]{0,1:T(8,128)S(1)}, s32[72,5]{0,1:T(8,128)}, u32[]{:S(2)}) copy-start(s32[72,5]{0,1:T(8,128)} %param.8) | copy-start | bytes 4324
  231.9 97.0 %all-reduce.5.cloned.1.call-start = ((), (), s32[]{:S(2)}) async-start(), calls=%async_computation.4 | async-start | bytes 131072 | tf_op jit(solution)/shard_map/psum | solution.py:62
  271.9 129.9 %all-gather.2.cloned.1.call-start = ((), (), s32[]{:S(2)}) async-start(), calls=%async_computation.5 | async-start | bytes 4718592 | tf_op jit(solution)/shard_map/all_gather | solution.py:69
  355.7 140.7 %reduce-scatter.2.cloned.1.call-start = ((), (), s32[]{:S(2)}) async-start(), calls=%async_computation.6 | async-start | bytes 1310720 | tf_op jit(solution)/shard_map/reduce_scatter | solution.py:77
  468.5 1.0 copy-start
Sparse Core Ops, SparseCore 0:
  232.0 39.8 all-reduce.2
  274.2 54.6 all-reduce.4
  355.9 45.9 all-gather.1
  469.6 26.7 reduce-scatter.1
